TPU v7x, 32 devices: a whole 2x2x4 slice. The times are simulated.
32 devices in a mesh: batch: 4 (over y, x), rows: 8 (over z, core).
Axes of the slice: x: 2, y: 2, z: 4, core: 2. Of those that a mesh axis runs over, the one named last changes fastest.
Arguments:
- features: bfloat16 [256, 8, 16, 2048], P('batch', 'rows'), may hold values from -6 to 6
- w_reduce: bfloat16 [2048, 512], P('rows'), may hold values from -0.125 to 0.125
- w_spatial: bfloat16 [4608, 512], P('rows'), may hold values from -0.09375 to 0.09375
- w_expand: bfloat16 [512, 2048], P('rows'), may hold values from -0.25 to 0.25
- query_weight: bfloat16 [2048, 512], P('rows'), may hold values from -0.125 to 0.125
- w_key: bfloat16 [2048, 512], P('rows'), may hold values from -0.125 to 0.125
- w_value: bfloat16 [2048, 512], P('rows'), may hold values from -0.125 to 0.125
- w_out: bfloat16 [512, 2048], P('rows'), may hold values from -0.5 to 0.5
- w_head: bfloat16 [4096, 80], P('rows'), may hold values from -0.09375 to 0.09375
- gain_a: float32 [512], replicated, may hold values from 0.1 to 1.9
- bias_a: float32 [512], replicated, may hold values from -0.5 to 0.5
- gain_b: float32 [512], replicated, may hold values from 0.1 to 1.9
- bias_b: float32 [512], replicated, may hold values from -0.5 to 0.5
- gain_c: float32 [2048], replicated, may hold values from 0.1 to 1.9
- bias_c: float32 [2048], replicated, may hold values from -0.5 to 0.5
- ln_gain: float32 [512], replicated, may hold values from 0.1 to 1.9
- ln_bias: float32 [512], replicated, may hold values from -0.5 to 0.5
- head_bias: float32 [80], replicated, may hold values from -1 to 1
- bank: bfloat16 [320, 2048], P(('batch', 'rows')), may hold values from -6 to 6
- piece_box: int32 [256, 8], P(('batch', 'rows')), may hold values from 0 to 127
- piece_clip: int32 [256, 8], P(('batch', 'rows')), may hold values from 0 to 63
- send_count: int32 [256], P(('batch', 'rows')), may hold values from 0 to 8, as said below
- sample_pos: int32 [256, 224], P(('batch', 'rows')), may hold values from 0 to 15
- sample_weight: float32 [256, 224], P(('batch', 'rows')), may hold values from 0.01 to 0.06
- win_start: int32 [4096], P(('batch', 'rows')), may hold values from 0 to 60, as said below
- win_len: int32 [4096], P(('batch', 'rows')), may hold values from 20 to 40, as said below
- prob_cotangent: float32 [4096, 80], P(('batch', 'rows')), may hold values from -6 to 6
Outputs:
- probs: float32 [4096, 80], P(('batch', 'rows'))
- features_grad: bfloat16 [256, 8, 16, 2048], P('batch', 'rows')
- w_reduce_grad: float32 [2048, 512], P('rows', 'batch')
- w_spatial_grad: float32 [4608, 512], P('rows', 'batch')
- w_expand_grad: float32 [512, 2048], P('rows', 'batch')
- w_query_grad: float32 [2048, 512], P('rows', 'batch')
- w_key_grad: float32 [2048, 512], P('rows', 'batch')
- w_value_grad: float32 [2048, 512], P('rows', 'batch')
- w_out_grad: float32 [512, 2048], P('rows', 'batch')
- w_head_grad: float32 [4096, 80], P('rows', 'batch')
- gain_a_grad: float32 [512], replicated
- bias_a_grad: float32 [512], replicated
- gain_b_grad: float32 [512], replicated
- bias_b_grad: float32 [512], replicated
- gain_c_grad: float32 [2048], replicated
- bias_c_grad: float32 [2048], replicated
- ln_gain_grad: float32 [512], replicated
- ln_bias_grad: float32 [512], replicated
- classifier_bias_gradient: float32 [80], replicated
Inputs may be any that keep to these rules, and one draw needn't show every extreme that they name: `send_count`: at most 8 live slots from one device to one owner; some device sends exactly 8 to some owner in every draw. `win_len`: every window holds 20 to 40 entries, some box's exactly 40. win_start + win_len <= 80.
All inputs are finite; a program needn't handle non-finite values.
Results may differ from a plain program's by a relative error of at most 0.024.
Values may be sent and summed in bfloat16 or wider, within the bound.
A program may use at most 256 MiB of HBM per device.

v0:
```python
import jax
import jax.numpy as jnp
from jax import lax
from jax.sharding import PartitionSpec as P


def padded(cells, sides, width):
    for axis, dim in sides:
        count = lax.axis_size(axis)
        ends = count - 1
        head = lax.slice_in_dim(cells, 0, width, axis=dim)
        tail = lax.slice_in_dim(cells, cells.shape[dim] - width, cells.shape[dim], axis=dim)
        cells = jnp.concatenate(
            [
                lax.ppermute(tail, axis, [(i, (i + 1) % count) for i in range(ends)]),
                cells,
                lax.ppermute(head, axis, [((i + 1) % count, i) for i in range(ends)]),
            ],
            axis=dim,
        )
    return cells


def split_up(value, dim, peers):
    shape = value.shape
    parts = value.reshape(*shape[:dim], peers, shape[dim] // peers, *shape[dim + 1 :])
    return jnp.moveaxis(parts, dim, 0)


def sum_at_owner(value, axis, dim):
    peers = lax.axis_size(axis)
    parts = lax.all_to_all(split_up(value, dim, peers), axis, 0, 0, tiled=True)
    return jnp.sum(parts.astype(jnp.float32), axis=0)


def side_by_side(arrays, axis, dim, along):
    ends, at = ([], 0)
    for a in arrays[:-1]:
        at += a.shape[along]
        ends.append(at)
    both = jnp.concatenate(arrays, axis=along)
    return tuple(jnp.split(sum_at_owner(both, axis, dim), ends, axis=along))


def tdot(left, right):
    return lax.dot_general(
        left, right, (((0,), (0,)), ((), ())), preferred_element_type=jnp.float32
    )


def ndot(left, right):
    return lax.dot_general(
        left, right, (((1,), (1,)), ((), ())), preferred_element_type=jnp.float32
    )


def silu_slope(value):
    sig = jax.nn.sigmoid(value)
    return sig * (1.0 + value * (1.0 - sig))


def normalize(field, total_count):
    sums, squares = lax.psum((jnp.sum(field, 0), jnp.sum(field * field, 0)), ("batch", "rows"))
    centre_value = sums / total_count
    inverse = lax.rsqrt(squares / total_count - centre_value * centre_value + 1e-05)
    return ((field - centre_value) * inverse, inverse)


def segment_totals(grad, normed):
    return lax.psum((jnp.sum(grad, 0), jnp.sum(grad * normed, 0)), ("batch", "rows"))


def norm_back(grad, normed, inverse, gain, shift_sum, gain_total_grad, total_count):
    return (
        gain * inverse * (grad - shift_sum / total_count - normed * gain_total_grad / total_count)
    )


def on_device(
    features,
    w_reduce,
    w_spatial,
    w_expand,
    query_weight,
    w_key,
    w_value,
    w_out,
    w_head,
    gain_a,
    bias_a,
    gain_b,
    bias_b,
    gain_c,
    bias_c,
    ln_gain,
    ln_bias,
    head_bias,
    bank,
    piece_box,
    piece_clip,
    send_count,
    sample_pos,
    sample_weight,
    win_start,
    win_len,
    prob_cotangent,
):
    owners = lax.axis_size("rows")
    clip_dev, row_dev, col_count, d_in = features.shape
    cell_count = clip_dev * row_dev * col_count
    total_count = cell_count * owners * lax.axis_size("batch")
    w_a, w_b, w_c, w_q, w_k, w_v, w_o, w_h = (
        lax.all_gather(w_reduce, "rows", axis=0, tiled=True),
        lax.all_gather(w_spatial, "rows", axis=0, tiled=True),
        lax.all_gather(w_expand, "rows", axis=0, tiled=True),
        lax.all_gather(query_weight, "rows", axis=0, tiled=True),
        lax.all_gather(w_key, "rows", axis=0, tiled=True),
        lax.all_gather(w_value, "rows", axis=0, tiled=True),
        lax.all_gather(w_out, "rows", axis=0, tiled=True),
        lax.all_gather(w_head, "rows", axis=0, tiled=True),
    )
    d_mid = w_a.shape[1]
    flat_x = features.reshape(cell_count, d_in)
    pre_a = jnp.dot(flat_x, w_a, preferred_element_type=jnp.float32)
    hat_a, inverse_a = normalize(pre_a, total_count)
    act_a = gain_a * hat_a + bias_a
    low_a = jax.nn.silu(act_a).astype(jnp.bfloat16)
    halo_a = padded(low_a.reshape(clip_dev, row_dev, col_count, d_mid), (("rows", 1),), 1)
    halo_a = jnp.pad(halo_a, ((0, 0), (0, 0), (1, 1), (0, 0)))
    window_a = jnp.concatenate(
        [
            halo_a[:, row_step : row_step + row_dev, col_step : col_step + col_count]
            for row_step in range(3)
            for col_step in range(3)
        ],
        axis=3,
    ).reshape(cell_count, 9 * d_mid)
    pre_b = jnp.dot(window_a, w_b, preferred_element_type=jnp.float32)
    hat_b, inverse_b = normalize(pre_b, total_count)
    act_b = gain_b * hat_b + bias_b
    low_b = jax.nn.silu(act_b).astype(jnp.bfloat16)
    pre_c = jnp.dot(low_b, w_c, preferred_element_type=jnp.float32)
    hat_c, inverse_c = normalize(pre_c, total_count)
    pre_out = gain_c * hat_c + bias_c + flat_x.astype(jnp.float32)
    fmap = jax.nn.silu(pre_out).astype(jnp.bfloat16)
    capacity = piece_box.shape[1]
    samples = sample_pos.shape[1] // capacity
    slot_count = owners * capacity
    sample_cells = (
        piece_clip[:, :, None] * (row_dev * col_count)
        + sample_pos.reshape(owners, capacity, samples)
    ).reshape(slot_count, samples)
    is_live = (jnp.arange(capacity)[None, :] < send_count[:, None]).reshape(slot_count)
    slot_weights = sample_weight.reshape(slot_count, samples) * is_live[:, None].astype(jnp.float32)
    cell_ids = jnp.arange(cell_count)[None, :]
    interp_sum = jnp.zeros((slot_count, cell_count), jnp.float32)
    for sample_index in range(samples):
        interp_sum = interp_sum + jnp.where(
            sample_cells[:, sample_index, None] == cell_ids,
            slot_weights[:, sample_index, None],
            0.0,
        )
    interpolated_value = interp_sum.astype(jnp.bfloat16)
    region_parts = (
        jnp.dot(interpolated_value, fmap, preferred_element_type=jnp.float32)
        .astype(jnp.bfloat16)
        .reshape(owners, capacity, d_in)
    )
    arrived, arrived_box = (
        lax.all_to_all(region_parts, "rows", split_axis=0, concat_axis=0, tiled=True),
        lax.all_to_all(piece_box, "rows", split_axis=0, concat_axis=0, tiled=True),
    )
    box_dev = win_start.shape[0]
    flat_box = arrived_box.reshape(slot_count)
    owner_hits = (flat_box[None, :] == jnp.arange(box_dev)[:, None]).astype(jnp.bfloat16)
    pooled = jnp.dot(
        owner_hits, arrived.reshape(slot_count, d_in), preferred_element_type=jnp.float32
    )
    pooled_low = pooled.astype(jnp.bfloat16)
    keys_own = jnp.dot(bank, w_k, preferred_element_type=jnp.float32).astype(jnp.bfloat16)
    values_own = jnp.dot(bank, w_v, preferred_element_type=jnp.float32).astype(jnp.bfloat16)
    key_rows, value_rows = (
        lax.all_gather(keys_own, "rows", axis=0, tiled=True),
        lax.all_gather(values_own, "rows", axis=0, tiled=True),
    )
    bank_length = key_rows.shape[0]
    queries = jnp.dot(pooled_low, w_q, preferred_element_type=jnp.float32).astype(jnp.bfloat16)
    score_scale = d_mid ** (-0.5)
    scores = ndot(queries, key_rows) * score_scale
    positions = jnp.arange(bank_length)[None, :]
    window_mask = (positions >= win_start[:, None]) & (positions < (win_start + win_len)[:, None])
    attend = jax.nn.softmax(jnp.where(window_mask, scores, -1e30), axis=-1)
    attend_low = attend.astype(jnp.bfloat16)
    mixture = jnp.dot(attend_low, value_rows, preferred_element_type=jnp.float32)
    centred = mixture - jnp.mean(mixture, axis=-1, keepdims=True)
    inverse_z = lax.rsqrt(jnp.mean(centred * centred, axis=-1, keepdims=True) + 1e-05)
    hat_z = centred * inverse_z
    pre_ln = ln_gain * hat_z + ln_bias
    low_r = jax.nn.silu(pre_ln).astype(jnp.bfloat16)
    branch = jnp.dot(low_r, w_o, preferred_element_type=jnp.float32)
    joined = jnp.concatenate([pooled, pooled + branch], axis=1).astype(jnp.bfloat16)
    logits = jnp.dot(joined, w_h, preferred_element_type=jnp.float32) + head_bias
    likely = jax.nn.sigmoid(logits)
    d_logit = (prob_cotangent * (likely * (1.0 - likely))).astype(jnp.bfloat16)
    grad_head_bias = jnp.sum(d_logit.astype(jnp.float32), 0)
    grad_wh = tdot(joined, d_logit)
    d_joined = ndot(d_logit, w_h)
    d_pooled = d_joined[:, :d_in] + d_joined[:, d_in:]
    d_branch = d_joined[:, d_in:].astype(jnp.bfloat16)
    grad_wo = tdot(low_r, d_branch)
    d_ln = ndot(d_branch, w_o) * silu_slope(pre_ln)
    grad_ln_gain = jnp.sum(d_ln * hat_z, 0)
    grad_ln_bias = jnp.sum(d_ln, 0)
    d_hat = d_ln * ln_gain
    d_mixture = (
        inverse_z
        * (
            d_hat
            - jnp.mean(d_hat, axis=-1, keepdims=True)
            - hat_z * jnp.mean(d_hat * hat_z, axis=-1, keepdims=True)
        )
    ).astype(jnp.bfloat16)
    d_attend = ndot(d_mixture, value_rows)
    d_values = tdot(attend_low, d_mixture)
    d_scores = (attend * (d_attend - jnp.sum(d_attend * attend, axis=-1, keepdims=True))).astype(
        jnp.bfloat16
    )
    d_queries = (
        jnp.dot(d_scores, key_rows, preferred_element_type=jnp.float32) * score_scale
    ).astype(jnp.bfloat16)
    d_keys = tdot(d_scores, queries) * score_scale
    grad_wq = tdot(pooled_low, d_queries)
    d_pooled = d_pooled + ndot(d_queries, w_q)
    key_sum, value_sum = side_by_side(
        (d_keys.astype(jnp.bfloat16), d_values.astype(jnp.bfloat16)), "rows", 0, 1
    )
    grad_wk = tdot(bank, key_sum.astype(jnp.bfloat16))
    grad_wv = tdot(bank, value_sum.astype(jnp.bfloat16))
    back_pieces = jnp.take(d_pooled.astype(jnp.bfloat16), flat_box, axis=0).reshape(
        owners, capacity, d_in
    )
    returned = lax.all_to_all(back_pieces, "rows", split_axis=0, concat_axis=0, tiled=True)
    d_fmap = tdot(interpolated_value, returned.reshape(slot_count, d_in))
    d_pre = d_fmap * silu_slope(pre_out)
    head_sums = lax.psum(
        (jnp.sum(d_pre, 0), jnp.sum(d_pre * hat_c, 0), grad_ln_gain, grad_ln_bias, grad_head_bias),
        ("batch", "rows"),
    )
    d_c = norm_back(
        d_pre, hat_c, inverse_c, gain_c, head_sums[0], head_sums[1], total_count
    ).astype(jnp.bfloat16)
    grad_wc = tdot(low_b, d_c)
    d_act_b = ndot(d_c, w_c) * silu_slope(act_b)
    shift_b_sum, gain_b_sum = segment_totals(d_act_b, hat_b)
    d_b = norm_back(d_act_b, hat_b, inverse_b, gain_b, shift_b_sum, gain_b_sum, total_count).astype(
        jnp.bfloat16
    )
    grad_wb = tdot(window_a, d_b)
    halo_d = padded(d_b.reshape(clip_dev, row_dev, col_count, d_mid), (("rows", 1),), 1)
    halo_d = jnp.pad(halo_d, ((0, 0), (0, 0), (1, 1), (0, 0)))
    window_d = jnp.concatenate(
        [
            halo_d[
                :, 2 - row_step : 2 - row_step + row_dev, 2 - col_step : 2 - col_step + col_count
            ]
            for row_step in range(3)
            for col_step in range(3)
        ],
        axis=3,
    ).reshape(cell_count, 9 * d_mid)
    flipped = w_b.reshape(9, d_mid, d_mid).transpose(0, 2, 1).reshape(9 * d_mid, d_mid)
    d_act_a = jnp.dot(window_d, flipped, preferred_element_type=jnp.float32) * silu_slope(act_a)
    shift_a_sum, gain_a_sum = segment_totals(d_act_a, hat_a)
    d_a = norm_back(d_act_a, hat_a, inverse_a, gain_a, shift_a_sum, gain_a_sum, total_count).astype(
        jnp.bfloat16
    )
    grad_wa = tdot(flat_x, d_a)
    grad_input = (ndot(d_a, w_a) + d_pre).astype(jnp.bfloat16).reshape(features.shape)
    partial_sums = (
        lax.psum_scatter(grad_wa, "rows", scatter_dimension=0, tiled=True),
        lax.psum_scatter(grad_wb, "rows", scatter_dimension=0, tiled=True),
        lax.psum_scatter(grad_wc, "rows", scatter_dimension=0, tiled=True),
        lax.psum_scatter(grad_wq, "rows", scatter_dimension=0, tiled=True),
        lax.psum_scatter(grad_wk, "rows", scatter_dimension=0, tiled=True),
        lax.psum_scatter(grad_wv, "rows", scatter_dimension=0, tiled=True),
        lax.psum_scatter(grad_wo, "rows", scatter_dimension=0, tiled=True),
        lax.psum_scatter(grad_wh, "rows", scatter_dimension=0, tiled=True),
    )
    finished = (
        lax.psum_scatter(
            partial_sums[0].astype(jnp.bfloat16), "batch", scatter_dimension=1, tiled=True
        ).astype(jnp.float32),
        lax.psum_scatter(
            partial_sums[1].astype(jnp.bfloat16), "batch", scatter_dimension=1, tiled=True
        ).astype(jnp.float32),
        lax.psum_scatter(
            partial_sums[2].astype(jnp.bfloat16), "batch", scatter_dimension=1, tiled=True
        ).astype(jnp.float32),
        lax.psum_scatter(
            partial_sums[3].astype(jnp.bfloat16), "batch", scatter_dimension=1, tiled=True
        ).astype(jnp.float32),
        lax.psum_scatter(
            partial_sums[4].astype(jnp.bfloat16), "batch", scatter_dimension=1, tiled=True
        ).astype(jnp.float32),
        lax.psum_scatter(
            partial_sums[5].astype(jnp.bfloat16), "batch", scatter_dimension=1, tiled=True
        ).astype(jnp.float32),
        lax.psum_scatter(
            partial_sums[6].astype(jnp.bfloat16), "batch", scatter_dimension=1, tiled=True
        ).astype(jnp.float32),
        lax.psum_scatter(
            partial_sums[7].astype(jnp.bfloat16), "batch", scatter_dimension=1, tiled=True
        ).astype(jnp.float32),
    )
    return (
        likely,
        grad_input,
        finished[0],
        finished[1],
        finished[2],
        finished[3],
        finished[4],
        finished[5],
        finished[6],
        finished[7],
        gain_a_sum,
        shift_a_sum,
        gain_b_sum,
        shift_b_sum,
        head_sums[1],
        head_sums[0],
        head_sums[2],
        head_sums[3],
        head_sums[4],
    )


def solution(mesh):
    return jax.shard_map(
        on_device,
        mesh=mesh,
        in_specs=(
            P("batch", "rows", None, None),
            P("rows", None),
            P("rows", None),
            P("rows", None),
            P("rows", None),
            P("rows", None),
            P("rows", None),
            P("rows", None),
            P("rows", None),
            P(),
            P(),
            P(),
            P(),
            P(),
            P(),
            P(),
            P(),
            P(),
            P(("batch", "rows"), None),
            P(("batch", "rows"), None),
            P(("batch", "rows"), None),
            P(("batch", "rows")),
            P(("batch", "rows"), None),
            P(("batch", "rows"), None),
            P(("batch", "rows")),
            P(("batch", "rows")),
            P(("batch", "rows"), None),
        ),
        out_specs=(
            P(("batch", "rows"), None),
            P("batch", "rows", None, None),
            P("rows", "batch"),
            P("rows", "batch"),
            P("rows", "batch"),
            P("rows", "batch"),
            P("rows", "batch"),
            P("rows", "batch"),
            P("rows", "batch"),
            P("rows", "batch"),
            P(),
            P(),
            P(),
            P(),
            P(),
            P(),
            P(),
            P(),
            P(),
        ),
        check_vma=False,
    )
```

profile of v0, /device:TPU:0, one launch (start us, length us, event | category | flops | bytes accessed | tf_op | source)
XLA Modules:
  0.0 1011.4 jit_solution(11663919438469440399)
XLA Ops:
  11.2 6.3 all-to-all-start
  19.9 21.7 %all-gather.10.cloned.1.call-done = bf16[2048,512]{1,0:T(8,128)(2,1)} async-done(((bf16[256,512]{1,0:T(8,128)(2,1)}), bf16[2048,512]{1,0:T(8,128)(2,1)}) %all-gather.10.cloned.1.call-update) | async-done | bytes 2097168 | tf_op jit(solution)/shard_map/all_gather | solution.py:113
  41.6 5.2 fusion.49
  46.9 42.2 %all-reduce.8 = (f32[512]{0:T(512)S(1)}, f32[512]{0:T(512)S(1)}) all-reduce(f32[512]{0:T(512)S(1)} %get-tuple-element.106, f32[512]{0:T(512)S(1)} %get-tuple-element.105), channel_id=1, replica_groups=mesh['batch'=4,'rows'=8] {'batch','rows'}, use_global_device_ids=true, to_apply=%region_3.0 | all-reduce | flops 1024 | bytes 8192 | tf_op jit(solution)/shard_map/psum | solution.py:63
  97.0 39.7 %all_gather.39 = bf16[4096,80]{0,1:T(8,128)(2,1)} all-gather(bf16[512,80]{0,1:T(8,128)(2,1)S(1)} %copy-done.8), channel_id=1, replica_groups=mesh['batch'=4,'rows'=8] {'rows'}, dimensions={0}, use_global_device_ids=true | all-gather | bytes 737280 | tf_op jit(solution)/shard_map/all_gather | solution.py:120
  138.5 3.6 select_maximum_fusion.2
  157.1 10.1 %fusion.48 = (f32[512]{0:T(512)S(1)}, f32[512]{0:T(512)S(1)}, f32[1024,512]{1,0:T(8,128)}) fusion(bf16[1024,4608]{1,0:T(8,128)(2,1)} %constant_dynamic-update-slice_fusion, bf16[4608,512]{1,0:T(8,128)(2,1)} %all-gather.12.cloned.1.call-done), kind=kOutput, calls=%fused_computation.239 | convolution fusion | flops 4833410048 | bytes 16257024 | tf_op jit(solution)/shard_map/dot_general | solution.py:138
  167.2 41.5 %all-reduce.7 = (f32[512]{0:T(512)S(1)}, f32[512]{0:T(512)S(1)}) all-reduce(f32[512]{0:T(512)S(1)} %get-tuple-element.104, f32[512]{0:T(512)S(1)} %get-tuple-element.103), channel_id=1, replica_groups=mesh['batch'=4,'rows'=8] {'batch','rows'}, use_global_device_ids=true, to_apply=%region_7.8 | all-reduce | flops 1024 | bytes 8192 | tf_op jit(solution)/shard_map/psum | solution.py:63
  208.9 8.2 fusion.45
  217.0 42.3 %all-reduce.6 = (f32[2048]{0:T(1024)S(1)}, f32[2048]{0:T(1024)S(1)}) all-reduce(f32[2048]{0:T(1024)S(1)} %get-tuple-element.98, f32[2048]{0:T(1024)S(1)} %get-tuple-element.97), channel_id=1, replica_groups=mesh['batch'=4,'rows'=8] {'batch','rows'}, use_global_device_ids=true, to_apply=%region_11.12 | all-reduce | flops 4096 | bytes 32768 | tf_op jit(solution)/shard_map/psum | solution.py:63
  259.8 10.3 %fusion.6 = bf16[8,8,2048]{2,1,0:T(8,128)(2,1)} fusion(bf16[1024,2048]{1,0:T(8,128)(2,1)} %bitcast.110, f32[2048]{0:T(1024)S(1)} %copy-done.116, f32[2048]{0:T(1024)S(1)} %get-tuple-element.197, f32[1024,2048]{1,0:T(8,128)} %get-tuple-element.207, f32[2048]{0:T(1024)S(1)} %get-tuple-element.198, f32[2048]{0:T(1024)S(1)} %copy-done.20, ...), kind=kOutput, calls=%fused_computation.27 | convolution fusion | flops 297140224 | bytes 12892160 | tf_op jit(solution)/shard_map/dot_general | solution.py:165
  270.1 3.4 all-to-all-start.1
  275.5 15.3 %all-gather = bf16[8,10,512]{2,1,0:T(8,128)(2,1)S(1)} all-gather(bf16[1,10,512]{2,1,0:T(8,128)(2,1)S(1)} %fusion.14), channel_id=1, replica_groups=mesh['batch'=4,'rows'=8] {'rows'}, dimensions={0}, use_global_device_ids=true | all-gather | bytes 92160 | tf_op jit(solution)/shard_map/all_gather | solution.py:183
  292.9 14.4 %all-gather.1 = bf16[8,10,512]{2,1,0:T(8,128)(2,1)S(1)} all-gather(bf16[1,10,512]{2,1,0:T(8,128)(2,1)S(1)} %fusion.15), channel_id=1, replica_groups=mesh['batch'=4,'rows'=8] {'rows'}, dimensions={0}, use_global_device_ids=true | all-gather | bytes 92160 | tf_op jit(solution)/shard_map/all_gather | solution.py:184
  313.9 2.8 convert_reduce_fusion
  321.0 3.1 multiply_reduce_fusion.6
  324.8 2.7 fusion.58
  327.6 4.1 fusion.20
  332.2 16.3 %all_to_all.24 = bf16[8,10,1024]{2,1,0:T(8,128)(2,1)S(1)} all-to-all(bf16[8,10,1024]{2,1,0:T(8,128)(2,1)S(1)} %reshape.231), channel_id=1, replica_groups=mesh['batch'=4,'rows'=8] {'rows'}, dimensions={0} | all-to-all | bytes 327680 | tf_op jit(solution)/shard_map/all_to_all | solution.py:32
  348.6 2.7 convolution_bitcast_fusion.1
  354.7 3.0 fusion.4
  358.5 17.0 %all_to_all.25 = bf16[8,8,2048]{2,1,0:T(8,128)(2,1)S(1)} all-to-all(bf16[8,8,2048]{2,1,0:T(8,128)(2,1)S(1)} %bitcast_select_fusion), channel_id=1, replica_groups=mesh['batch'=4,'rows'=8] {'rows'}, dimensions={0} | all-to-all | bytes 524288 | tf_op jit(solution)/shard_map/all_to_all | solution.py:242
  375.9 14.8 %fusion.44 = (f32[2048]{0:T(1024)S(1)}, f32[2048]{0:T(1024)S(1)}, f32[1024,2048]{1,0:T(8,128)}) fusion(f32[2048]{0:T(1024)S(1)} %get-tuple-element.197, f32[1024,2048]{1,0:T(8,128)} %get-tuple-element.207, f32[2048]{0:T(1024)S(1)} %get-tuple-element.198, bf16[1024,2048]{1,0:T(8,128)(2,1)} %bitcast.111, f32[2048]{0:T(1024)} %param.41, ...), kind=kOutput, calls=%fused_computation.235 | convolution fusion | flops 309587968 | bytes 21297152 | tf_op jit(solution)/shard_map/dot_general | solution.py:46
  390.7 38.9 %all-reduce.5 = (f32[2048]{0:T(1024)S(1)}, f32[2048]{0:T(1024)S(1)}) all-reduce(f32[2048]{0:T(1024)S(1)} %get-tuple-element.96, f32[2048]{0:T(1024)S(1)} %get-tuple-element.95), channel_id=1, replica_groups=mesh['batch'=4,'rows'=8] {'batch','rows'}, use_global_device_ids=true, to_apply=%region_22.23 | all-reduce | flops 4096 | bytes 32768 | tf_op jit(solution)/shard_map/psum | solution.py:245
  429.7 7.4 multiply_convert_fusion
  439.2 4.6 fusion.42
  444.0 8.1 fusion.47
  452.1 42.8 %all-reduce.4 = (f32[512]{0:T(512)S(1)}, f32[512]{0:T(512)S(1)}) all-reduce(f32[512]{0:T(512)S(1)} %get-tuple-element.102, f32[512]{0:T(512)S(1)} %get-tuple-element.101), channel_id=1, replica_groups=mesh['batch'=4,'rows'=8] {'batch','rows'}, use_global_device_ids=true, to_apply=%region_26.27 | all-reduce | flops 1024 | bytes 8192 | tf_op jit(solution)/shard_map/psum | solution.py:70
  494.8 2.9 multiply_convert_fusion.8
  497.7 2.7 collective-permute-start.2
  501.7 6.7 copy.62
  508.4 3.6 select_maximum_fusion
  518.0 7.1 fusion.46
  525.2 53.3 %all-reduce.3 = (f32[512]{0:T(512)S(1)}, f32[512]{0:T(512)S(1)}, f32[512]{0:T(512)}, f32[512]{0:T(512)}, f32[80]{0:T(128)}) all-reduce(f32[512]{0:T(512)S(1)} %get-tuple-element.100, f32[512]{0:T(512)S(1)} %get-tuple-element.99, f32[512]{0:T(512)S(1)} %copy-done.28, ...), channel_id=1, replica_groups=mesh['batch'=4,'rows'=8] {'batch','rows'}, use_global_device_ids=true, to_apply=%region_30.31 | all-reduce | flops 2128 | bytes 17024 | tf_op jit(solution)/shard_map/psum | solution.py:70
  581.8 4.4 convolution_bitcast_fusion.2
  586.3 11.4 %fusion.57 = f32[4608,512]{1,0:T(8,128)} fusion(bf16[1024,4608]{1,0:T(8,128)(2,1)} %constant_dynamic-update-slice_fusion, bf16[1024,512]{1,0:T(8,128)(2,1)S(1)} %multiply_convert_fusion.8), kind=kOutput, calls=%fused_computation.247 | convolution fusion | flops 4831838208 | bytes 19922944 | tf_op jit(solution)/shard_map/dot_general | solution.py:46
  607.2 10.4 %reduce-scatter.26.cloned.1.call-done = f32[64,2048]{1,0:T(8,128)} async-done(((f32[512,2048]{1,0:T(8,128)}), f32[64,2048]{1,0:T(8,128)}) %reduce-scatter.26.cloned.1.call-update) | async-done | bytes 524304 | tf_op jit(solution)/shard_map/reduce_scatter | solution.py:282
  619.5 49.1 %reduce-scatter.20.cloned.1.call-done = f32[256,512]{0,1:T(8,128)} async-done(((f32[2048,512]{0,1:T(8,128)}), f32[256,512]{0,1:T(8,128)}) %reduce-scatter.20.cloned.1.call-update) | async-done | bytes 524304 | tf_op jit(solution)/shard_map/reduce_scatter | solution.py:280
  670.4 98.0 %reduce-scatter.24.cloned.1.call-done = f32[576,512]{1,0:T(8,128)} async-done(((f32[4608,512]{1,0:T(8,128)}), f32[576,512]{1,0:T(8,128)}) %reduce-scatter.24.cloned.1.call-update) | async-done | bytes 1179664 | tf_op jit(solution)/shard_map/reduce_scatter | solution.py:281
  772.2 8.5 add_convert_fusion
  780.7 30.6 %all-reduce.11.cloned.1.call-done = bf16[512,80]{0,1:T(8,128)(2,1)} async-done(((bf16[512,80]{0,1:T(8,128)(2,1)}), bf16[512,80]{0,1:T(8,128)(2,1)}) %all-reduce.11.cloned.1.call-update) | async-done | bytes 81936
  812.6 26.3 %reduce-scatter.48.cloned.1.call-done = bf16[128,256]{1,0:T(8,128)(2,1)} async-done(((bf16[512,256]{1,0:T(8,128)(2,1)}), bf16[128,256]{1,0:T(8,128)(2,1)}) %reduce-scatter.48.cloned.1.call-update) | async-done | bytes 65552
  840.5 25.1 %reduce-scatter.42.cloned.1.call-done = bf16[64,512]{1,0:T(8,128)(2,1)} async-done(((bf16[64,2048]{1,0:T(8,128)(2,1)}), bf16[64,512]{1,0:T(8,128)(2,1)}) %reduce-scatter.42.cloned.1.call-update) | async-done | bytes 65552 | tf_op jit(solution)/shard_map/reduce_scatter | solution.py:308
  867.2 25.6 %reduce-scatter.34.cloned.1.call-done = bf16[256,128]{0,1:T(8,128)(2,1)} async-done(((bf16[256,512]{0,1:T(8,128)(2,1)}), bf16[256,128]{0,1:T(8,128)(2,1)}) %reduce-scatter.34.cloned.1.call-update) | async-done | bytes 65552 | tf_op jit(solution)/shard_map/reduce_scatter | solution.py:302
  894.4 25.1 %reduce-scatter.38.cloned.1.call-done = bf16[256,128]{0,1:T(8,128)(2,1)} async-done(((bf16[256,512]{0,1:T(8,128)(2,1)}), bf16[256,128]{0,1:T(8,128)(2,1)}) %reduce-scatter.38.cloned.1.call-update) | async-done | bytes 65552 | tf_op jit(solution)/shard_map/reduce_scatter | solution.py:305
  921.1 25.5 %reduce-scatter.28.cloned.1.call-done = bf16[64,512]{1,0:T(8,128)(2,1)} async-done(((bf16[64,2048]{1,0:T(8,128)(2,1)}), bf16[64,512]{1,0:T(8,128)(2,1)}) %reduce-scatter.28.cloned.1.call-update) | async-done | bytes 65552 | tf_op jit(solution)/shard_map/reduce_scatter | solution.py:296
  948.1 26.0 %reduce-scatter.22.cloned.1.call-done = bf16[256,128]{0,1:T(8,128)(2,1)} async-done(((bf16[256,512]{0,1:T(8,128)(2,1)}), bf16[256,128]{0,1:T(8,128)(2,1)}) %reduce-scatter.22.cloned.1.call-update) | async-done | bytes 65552 | tf_op jit(solution)/shard_map/reduce_scatter | solution.py:290
  975.6 27.0 %reduce-scatter.46.cloned.1.call-done = bf16[128,576]{1,0:T(8,128)(2,1)} async-done(((bf16[512,576]{1,0:T(8,128)(2,1)}), bf16[128,576]{1,0:T(8,128)(2,1)}) %reduce-scatter.46.cloned.1.call-update) | async-done | bytes 147472
  (412 shorter events, 92.2 us)
Async XLA Ops:
  7.2 266.4 %copy-start = (bf16[10,2048]{1,0:T(8,128)(2,1)S(1)}, bf16[10,2048]{1,0:T(8,128)(2,1)}, u32[]{:S(2)}) copy-start(bf16[10,2048]{1,0:T(8,128)(2,1)} %param.45) | copy-start | bytes 122884
  7.2 34.4 %all-gather.10.cloned.1.call-start = ((), (), s32[]{:S(2)}) async-start(), calls=%async_computation.19 | async-start | bytes 2359296 | tf_op jit(solution)/shard_map/all_gather | solution.py:113
  7.9 149.2 %all-gather.12.cloned.1.call-start = ((), (), s32[]{:S(2)}) async-start(), calls=%async_computation.20 | async-start | bytes 5308416 | tf_op jit(solution)/shard_map/all_gather | solution.py:114
  8.7 200.1 %all-gather.14.cloned.1.call-start = ((), (), s32[]{:S(2)}) async-start(), calls=%async_computation.21 | async-start | bytes 2359296 | tf_op jit(solution)/shard_map/all_gather | solution.py:115
  9.4 264.1 %all-gather.18.cloned.1.call-start = ((), (), s32[]{:S(2)}) async-start(), calls=%async_computation.23 | async-start | bytes 2359296 | tf_op jit(solution)/shard_map/all_gather | solution.py:117
  10.0 280.9 %all-gather.20.cloned.1.call-start = ((), (), s32[]{:S(2)}) async-start(), calls=%async_computation.24 | async-start | bytes 2359296 | tf_op jit(solution)/shard_map/all_gather | solution.py:118
  10.6 298.0 %all-gather.16.cloned.1.call-start = ((), (), s32[]{:S(2)}) async-start(), calls=%async_computation.22 | async-start | bytes 2359296 | tf_op jit(solution)/shard_map/all_gather | solution.py:116
  11.2 126.1 %all-to-all-start = ((s32[8,1,8]{2,1,0:T(1,128)}), s32[8,1,8]{2,1,0:T(1,128)S(1)}, u32[]{:S(2)}, u32[]{:S(2)}) async-start(s32[8,1,8]{2,1,0:T(1,128)} %bitcast.138), calls=%async_computation | async-start | bytes 8192 | tf_op jit(solution)/shard_map/all_to_all | solution.py:171
  17.5 293.9 %all-gather.22.cloned.1.call-start = ((), (), s32[]{:S(2)}) async-start(), calls=%async_computation.25 | async-start | bytes 2359296 | tf_op jit(solution)/shard_map/all_gather | solution.py:119
  89.8 48.7 %collective-permute-start = (bf16[64,1,16,512]{3,2,0,1:T(8,128)(2,1)S(1)}, bf16[64,1,16,512]{3,2,0,1:T(8,128)(2,1)}, u32[]{:S(2)}, u32[]{:S(2)}) collective-permute-start(bf16[64,1,16,512]{3,2,0,1:T(8,128)(2,1)S(1)} %bitcast.117), channel_id=1, source_target_pairs={{0,1},{1,2},{2,3},{3,4},{4,5},{5,6},{6,7},{8,9},{9,10},{10,11},{11... | collective-permute-start | bytes 3145736 | tf_op jit(solution)/shard_map/ppermute | solution.py:15
  92.5 46.0 %collective-permute-start.1 = (bf16[64,1,16,512]{3,2,0,1:T(8,128)(2,1)S(1)}, bf16[64,1,16,512]{3,2,0,1:T(8,128)(2,1)}, u32[]{:S(2)}, u32[]{:S(2)}) collective-permute-start(bf16[64,1,16,512]{3,2,0,1:T(8,128)(2,1)S(1)} %bitcast.118), channel_id=1, source_target_pairs={{1,0},{2,1},{3,2},{4,3},{5,4},{6,5},{7,6},{9,8},{10,9},{11,10},{12... | collective-permute-start | bytes 3145736 | tf_op jit(solution)/shard_map/ppermute | solution.py:17
  94.4 165.0 %copy-start.35 = (s32[64]{0:T(128)}, s32[64]{0:T(128)S(1)}, u32[]{:S(2)}) copy-start(s32[64]{0:T(128)S(1)} %get-tuple-element.149) | copy-start | bytes 772
  94.4 165.0 %copy-start.37 = (s32[64]{0:T(128)}, s32[64]{0:T(128)S(1)}, u32[]{:S(2)}) copy-start(s32[64]{0:T(128)S(1)} %get-tuple-element.150) | copy-start | bytes 772
  94.4 165.0 %copy-start.39 = (s32[64]{0:T(128)}, s32[64]{0:T(128)S(1)}, u32[]{:S(2)}) copy-start(s32[64]{0:T(128)S(1)} %get-tuple-element.151) | copy-start | bytes 772
  94.4 165.0 %copy-start.41 = (s32[64]{0:T(128)}, s32[64]{0:T(128)S(1)}, u32[]{:S(2)}) copy-start(s32[64]{0:T(128)S(1)} %get-tuple-element.152) | copy-start | bytes 772
  94.4 165.0 %copy-start.43 = (s32[64]{0:T(128)}, s32[64]{0:T(128)S(1)}, u32[]{:S(2)}) copy-start(s32[64]{0:T(128)S(1)} %get-tuple-element.153) | copy-start | bytes 772
  94.5 165.0 %copy-start.45 = (s32[64]{0:T(128)}, s32[64]{0:T(128)S(1)}, u32[]{:S(2)}) copy-start(s32[64]{0:T(128)S(1)} %get-tuple-element.154) | copy-start | bytes 772
  94.5 165.0 %copy-start.47 = (s32[64]{0:T(128)}, s32[64]{0:T(128)S(1)}, u32[]{:S(2)}) copy-start(s32[64]{0:T(128)S(1)} %get-tuple-element.155) | copy-start | bytes 772
  94.5 165.0 %copy-start.49 = (s32[64]{0:T(128)}, s32[64]{0:T(128)S(1)}, u32[]{:S(2)}) copy-start(s32[64]{0:T(128)S(1)} %get-tuple-element.156) | copy-start | bytes 772
  94.5 165.0 %copy-start.51 = (s32[64]{0:T(128)}, s32[64]{0:T(128)S(1)}, u32[]{:S(2)}) copy-start(s32[64]{0:T(128)S(1)} %get-tuple-element.157) | copy-start | bytes 772
  95.7 163.9 %copy-start.83 = (s32[64]{0:T(128)}, s32[64]{0:T(128)S(1)}, u32[]{:S(2)}) copy-start(s32[64]{0:T(128)S(1)} %get-tuple-element.116) | copy-start | bytes 772
  95.7 163.9 %copy-start.85 = (s32[64]{0:T(128)}, s32[64]{0:T(128)S(1)}, u32[]{:S(2)}) copy-start(s32[64]{0:T(128)S(1)} %get-tuple-element.117) | copy-start | bytes 772
  95.7 163.9 %copy-start.87 = (s32[64]{0:T(128)}, s32[64]{0:T(128)S(1)}, u32[]{:S(2)}) copy-start(s32[64]{0:T(128)S(1)} %get-tuple-element.118) | copy-start | bytes 772
  95.7 163.9 %copy-start.89 = (s32[64]{0:T(128)}, s32[64]{0:T(128)S(1)}, u32[]{:S(2)}) copy-start(s32[64]{0:T(128)S(1)} %get-tuple-element.119) | copy-start | bytes 772
  95.7 163.9 %copy-start.91 = (s32[64]{0:T(128)}, s32[64]{0:T(128)S(1)}, u32[]{:S(2)}) copy-start(s32[64]{0:T(128)S(1)} %get-tuple-element.120) | copy-start | bytes 772
  95.7 163.9 %copy-start.93 = (s32[64]{0:T(128)}, s32[64]{0:T(128)S(1)}, u32[]{:S(2)}) copy-start(s32[64]{0:T(128)S(1)} %get-tuple-element.121) | copy-start | bytes 772
  270.1 37.2 %all-to-all-start.1 = ((bf16[8,8,2048]{2,1,0:T(8,128)(2,1)}), bf16[8,8,2048]{2,1,0:T(8,128)(2,1)S(1)}, u32[]{:S(2)}, u32[]{:S(2)}) async-start(bf16[8,8,2048]{2,1,0:T(8,128)(2,1)} %fusion.6), calls=%async_computation.1 | async-start | bytes 524288 | tf_op jit(solution)/shard_map/all_to_all | solution.py:170
  273.5 324.3 %reduce-scatter.44.cloned.1.call-start = ((), (), s32[]{:S(2)}) async-start(), calls=%async_computation.38 | async-start | bytes 1474560 | tf_op jit(solution)/shard_map/reduce_scatter | solution.py:287
  318.1 281.4 %reduce-scatter.30.cloned.1.call-start = ((), (), s32[]{:S(2)}) async-start(), calls=%async_computation.31 | async-start | bytes 4718592 | tf_op jit(solution)/shard_map/reduce_scatter | solution.py:283
  327.5 274.0 %reduce-scatter.40.cloned.1.call-start = ((), (), s32[]{:S(2)}) async-start(), calls=%async_computation.36 | async-start | bytes 4718592 | tf_op jit(solution)/shard_map/reduce_scatter | solution.py:286
  331.8 271.6 %reduce-scatter.32.cloned.1.call-start = ((), (), s32[]{:S(2)}) async-start(), calls=%async_computation.32 | async-start | bytes 4718592 | tf_op jit(solution)/shard_map/reduce_scatter | solution.py:284
  351.4 254.0 %reduce-scatter.36.cloned.1.call-start = ((), (), s32[]{:S(2)}) async-start(), calls=%async_computation.34 | async-start | bytes 4718592 | tf_op jit(solution)/shard_map/reduce_scatter | solution.py:285
  354.5 263.1 %reduce-scatter.26.cloned.1.call-start = ((), (), s32[]{:S(2)}) async-start(), calls=%async_computation.29 | async-start | bytes 4718592 | tf_op jit(solution)/shard_map/reduce_scatter | solution.py:282
  443.7 224.8 %reduce-scatter.20.cloned.1.call-start = ((), (), s32[]{:S(2)}) async-start(), calls=%async_computation.26 | async-start | bytes 4718592 | tf_op jit(solution)/shard_map/reduce_scatter | solution.py:280
  497.7 10.7 %collective-permute-start.2 = (bf16[64,1,16,512]{3,2,0,1:T(8,128)(2,1)S(1)}, bf16[64,1,16,512]{3,2,0,1:T(8,128)(2,1)}, u32[]{:S(2)}, u32[]{:S(2)}) collective-permute-start(bf16[64,1,16,512]{3,2,0,1:T(8,128)(2,1)S(1)} %bitcast.106), channel_id=1, source_target_pairs={{0,1},{1,2},{2,3},{3,4},{4,5},{5,6},{6,7},{8,9},{9,10},{10,11},{11... | collective-permute-start | bytes 3145736 | tf_op jit(solution)/shard_map/ppermute | solution.py:15
  500.4 8.0 collective-permute-start.3
  586.3 182.1 %reduce-scatter.24.cloned.1.call-start = ((), (), s32[]{:S(2)}) async-start(), calls=%async_computation.28 | async-start | bytes 10616832 | tf_op jit(solution)/shard_map/reduce_scatter | solution.py:281
  597.8 213.5 %all-reduce.11.cloned.1.call-start = ((), (), s32[]{:S(2)}) async-start(), calls=%async_computation.41 | async-start | bytes 163840
  599.4 239.5 %reduce-scatter.48.cloned.1.call-start = ((), (), s32[]{:S(2)}) async-start(), calls=%async_computation.40 | async-start | bytes 327680
  601.4 264.2 %reduce-scatter.42.cloned.1.call-start = ((), (), s32[]{:S(2)}) async-start(), calls=%async_computation.37 | async-start | bytes 327680 | tf_op jit(solution)/shard_map/reduce_scatter | solution.py:308
  603.3 167.6 %copy-start.121 = (u32[32]{0:T(128)S(1)}, u32[32]{0:T(128)}, u32[]{:S(2)}) copy-start(u32[32]{0:T(128)} %constant.85) | copy-start | bytes 388
  603.3 168.8 %copy-start.5 = (bf16[1024,512]{1,0:T(8,128)(2,1)S(1)}, bf16[1024,512]{1,0:T(8,128)(2,1)}, u32[]{:S(2)}) copy-start(bf16[1024,512]{1,0:T(8,128)(2,1)} %copy-done.4) | copy-start | bytes 3145732
  603.3 289.4 %reduce-scatter.34.cloned.1.call-start = ((), (), s32[]{:S(2)}) async-start(), calls=%async_computation.33 | async-start | bytes 327680 | tf_op jit(solution)/shard_map/reduce_scatter | solution.py:302
  605.3 314.1 %reduce-scatter.38.cloned.1.call-start = ((), (), s32[]{:S(2)}) async-start(), calls=%async_computation.35 | async-start | bytes 327680 | tf_op jit(solution)/shard_map/reduce_scatter | solution.py:305
  607.2 339.4 %reduce-scatter.28.cloned.1.call-start = ((), (), s32[]{:S(2)}) async-start(), calls=%async_computation.30 | async-start | bytes 327680 | tf_op jit(solution)/shard_map/reduce_scatter | solution.py:296
  619.4 354.6 %reduce-scatter.22.cloned.1.call-start = ((), (), s32[]{:S(2)}) async-start(), calls=%async_computation.27 | async-start | bytes 327680 | tf_op jit(solution)/shard_map/reduce_scatter | solution.py:290
  670.3 332.3 %reduce-scatter.46.cloned.1.call-start = ((), (), s32[]{:S(2)}) async-start(), calls=%async_computation.39 | async-start | bytes 819200
  772.1 232.3 %copy-start.1 = (bf16[10,2048]{1,0:T(8,128)(2,1)S(1)}, bf16[10,2048]{1,0:T(8,128)(2,1)}, u32[]{:S(2)}) copy-start(bf16[10,2048]{1,0:T(8,128)(2,1)} %param.45) | copy-start | bytes 122884
  (105 other events, 5091.6 us)
Sparse Core Ops, SparseCore 0:
  9.6 31.8 all-gather.9
  43.2 51.9 all-gather.11
  96.8 35.5 all-gather.13
  133.9 28.7 all-gather.17
  164.2 29.0 all-gather.19
  194.7 28.8 all-gather.15
  225.2 29.4 all-gather.21
  318.2 34.8 reduce-scatter.43
  355.4 53.8 reduce-scatter.29
  411.4 49.2 reduce-scatter.39
  463.0 51.3 reduce-scatter.31
  516.6 50.5 reduce-scatter.35
  569.4 48.1 reduce-scatter.25
  620.4 48.1 reduce-scatter.19
  670.7 97.6 reduce-scatter.23
  771.7 39.4 all-reduce.10
  814.1 24.8 reduce-scatter.47
  841.5 24.0 reduce-scatter.41
  868.6 24.0 reduce-scatter.33
  895.4 24.0 reduce-scatter.37
  922.4 24.0 reduce-scatter.27
  949.9 24.0 reduce-scatter.21
  977.2 25.3 reduce-scatter.45
where the time goes:
time: 1020 us; the launch traced here: 1010 us
  waiting for transfers between devices  395 us (39%)
  blocking collectives  364 us (36%)
  matrix products  128 us (13%)
  local copies, waits for them, and re-layouts  45.6 us (4%)
  other arithmetic  43.2 us (4%)
  starting transfers between devices  18.9 us (2%)
  between operations  17.1 us (2%)
    psum x3, blocking collectives, normalize(): lax.psum((jnp.sum(field, 0), jnp.sum(field * field, 0)), ('batch', 'rows'))  126 us
    reduce_scatter x1, waiting for transfers between devices, on_device(): lax.psum_scatter(grad_wb, 'rows', scatter_dimension=0, tiled=True)  98 us
    psum x2, blocking collectives, segment_totals(): lax.psum((jnp.sum(grad, 0), jnp.sum(grad * normed, 0)), ('batch', 'rows'))  96 us
    unnamed x26, waiting for transfers between devices  88.4 us
    dot_general x11, matrix products, tdot(): lax.dot_general(left, right, (((0,), (0,)), ((), ())), preferred_element_...  49.2 us
    reduce_scatter x1, waiting for transfers between devices, on_device(): lax.psum_scatter(grad_wa, 'rows', scatter_dimension=0, tiled=True)  49.1 us
    all_gather x1, blocking collectives, on_device(): lax.all_gather(w_head, 'rows', axis=0, tiled=True)  39.7 us
    psum x1, blocking collectives, on_device(): lax.psum((jnp.sum(d_pre, 0), jnp.sum(d_pre * hat_c, 0), grad_ln_gain, gra...  38.9 us
  transfers between devices with their start and end apart: 29, of which 12 were waited for; matrix products, arithmetic and copies ran while one was open for 20% of the time, Pallas kernels for 0%

commit v1 on v0

--- a/solution.py
+++ b/solution.py
@@ -60,7 +60,9 @@
 
 
 def normalize(field, total_count):
-    sums, squares = lax.psum((jnp.sum(field, 0), jnp.sum(field * field, 0)), ("batch", "rows"))
+    sums, squares = lax.psum(
+        lax.psum((jnp.sum(field, 0), jnp.sum(field * field, 0)), "rows"), "batch"
+    )
     centre_value = sums / total_count
     inverse = lax.rsqrt(squares / total_count - centre_value * centre_value + 1e-05)
     return ((field - centre_value) * inverse, inverse)

time: 1020 us -> 984 us (0.965)
  blocking collectives: 364 us -> 327 us
    psum x3 -> x6, blocking collectives: 126 us -> 90.4 us  [the longest x3 56.6 us: normalize(): lax.psum((jnp.sum(field, 0), jnp.sum(field * field, 0)), 'rows')]
    unnamed x273 -> x277, local copies, waits for them, and re-layouts: 28.3 us -> 28.3 us
  transfers between devices with their start and end apart: 29 -> 29, of which waited for: 12 -> 12; matrix products, arithmetic and copies ran while one was open for 20% -> 21% of each run, Pallas kernels for 0% -> 0%
where the time goes in v1:
time: 984 us; the launch traced here: 973 us
  waiting for transfers between devices  394 us (40%)
  blocking collectives  327 us (33%)
  matrix products  128 us (13%)
  local copies, waits for them, and re-layouts  45.6 us (5%)
  other arithmetic  43.2 us (4%)
  starting transfers between devices  18.8 us (2%)
  between operations  16.9 us (2%)
    reduce_scatter x1, waiting for transfers between devices, on_device(): lax.psum_scatter(grad_wb, 'rows', scatter_dimension=0, tiled=True)  98 us
    psum x2, blocking collectives, segment_totals(): lax.psum((jnp.sum(grad, 0), jnp.sum(grad * normed, 0)), ('batch', 'rows'))  94 us
    unnamed x26, waiting for transfers between devices  88.4 us
    psum x3, blocking collectives, normalize(): lax.psum((jnp.sum(field, 0), jnp.sum(field * field, 0)), 'rows')  56.6 us
    dot_general x11, matrix products, tdot(): lax.dot_general(left, right, (((0,), (0,)), ((), ())), preferred_element_...  49.2 us
    reduce_scatter x1, waiting for transfers between devices, on_device(): lax.psum_scatter(grad_wa, 'rows', scatter_dimension=0, tiled=True)  49 us
    psum x1, blocking collectives, on_device(): lax.psum((jnp.sum(d_pre, 0), jnp.sum(d_pre * hat_c, 0), grad_ln_gain, gra...  38.3 us
    all_gather x1, blocking collectives, on_device(): lax.all_gather(w_head, 'rows', axis=0, tiled=True)  35.5 us
  transfers between devices with their start and end apart: 29, of which 12 were waited for; matrix products, arithmetic and copies ran while one was open for 21% of the time, Pallas kernels for 0%

profile of v1, /device:TPU:0, one launch (start us, length us, event | category | flops | bytes accessed | tf_op | source)
XLA Modules:
  0.0 973.4 jit_solution(17122837557401892970)
XLA Ops:
  11.2 6.3 all-to-all-start
  19.9 21.7 %all-gather.10.cloned.1.call-done = bf16[2048,512]{1,0:T(8,128)(2,1)} async-done(((bf16[256,512]{1,0:T(8,128)(2,1)}), bf16[2048,512]{1,0:T(8,128)(2,1)}) %all-gather.10.cloned.1.call-update) | async-done | bytes 2097168 | tf_op jit(solution)/shard_map/all_gather | solution.py:115
  41.6 5.2 fusion.49
  46.9 15.9 %all-reduce.8 = (f32[512]{0:T(512)S(1)}, f32[512]{0:T(512)S(1)}) all-reduce(f32[512]{0:T(512)S(1)} %get-tuple-element.106, f32[512]{0:T(512)S(1)} %get-tuple-element.105), channel_id=1, replica_groups=mesh['batch'=4,'rows'=8] {'rows'}, use_global_device_ids=true, to_apply=%region_4.0 | all-reduce | flops 1024 | bytes 8192 | tf_op jit(solution)/shard_map/psum | solution.py:64
  62.8 9.8 %all-reduce.11 = (f32[512]{0:T(512)S(1)}, f32[512]{0:T(512)S(1)}) all-reduce(f32[512]{0:T(512)S(1)} %get-tuple-element.180, f32[512]{0:T(512)S(1)} %get-tuple-element.181), channel_id=1, replica_groups=mesh['batch'=4,'rows'=8] {'batch'}, use_global_device_ids=true, to_apply=%region_5.0 | all-reduce | flops 1024 | bytes 8192 | tf_op jit(solution)/shard_map/psum | solution.py:63
  80.1 35.5 %all_gather.39 = bf16[4096,80]{0,1:T(8,128)(2,1)} all-gather(bf16[512,80]{0,1:T(8,128)(2,1)S(1)} %copy-done.8), channel_id=1, replica_groups=mesh['batch'=4,'rows'=8] {'rows'}, dimensions={0}, use_global_device_ids=true | all-gather | bytes 737280 | tf_op jit(solution)/shard_map/all_gather | solution.py:122
  117.3 3.7 select_maximum_fusion.2
  135.9 10.1 %fusion.48 = (f32[512]{0:T(512)S(1)}, f32[512]{0:T(512)S(1)}, f32[1024,512]{1,0:T(8,128)}) fusion(bf16[1024,4608]{1,0:T(8,128)(2,1)} %constant_dynamic-update-slice_fusion, bf16[4608,512]{1,0:T(8,128)(2,1)} %all-gather.12.cloned.1.call-done), kind=kOutput, calls=%fused_computation.239 | convolution fusion | flops 4833410048 | bytes 16257024 | tf_op jit(solution)/shard_map/dot_general | solution.py:140
  146.0 14.4 %all-reduce.7 = (f32[512]{0:T(512)S(1)}, f32[512]{0:T(512)S(1)}) all-reduce(f32[512]{0:T(512)S(1)} %get-tuple-element.104, f32[512]{0:T(512)S(1)} %get-tuple-element.103), channel_id=1, replica_groups=mesh['batch'=4,'rows'=8] {'rows'}, use_global_device_ids=true, to_apply=%region_10.11 | all-reduce | flops 1024 | bytes 8192 | tf_op jit(solution)/shard_map/psum | solution.py:64
  160.4 10.1 %all-reduce.10 = (f32[512]{0:T(512)S(1)}, f32[512]{0:T(512)S(1)}) all-reduce(f32[512]{0:T(512)S(1)} %get-tuple-element.178, f32[512]{0:T(512)S(1)} %get-tuple-element.179), channel_id=1, replica_groups=mesh['batch'=4,'rows'=8] {'batch'}, use_global_device_ids=true, to_apply=%region_11.12 | all-reduce | flops 1024 | bytes 8192 | tf_op jit(solution)/shard_map/psum | solution.py:63
  170.6 8.3 fusion.45
  178.9 26.3 %all-reduce.6 = (f32[2048]{0:T(1024)S(1)}, f32[2048]{0:T(1024)S(1)}) all-reduce(f32[2048]{0:T(1024)S(1)} %get-tuple-element.98, f32[2048]{0:T(1024)S(1)} %get-tuple-element.97), channel_id=1, replica_groups=mesh['batch'=4,'rows'=8] {'rows'}, use_global_device_ids=true, to_apply=%region_16.17 | all-reduce | flops 4096 | bytes 32768 | tf_op jit(solution)/shard_map/psum | solution.py:64
  205.2 13.9 %all-reduce.9 = (f32[2048]{0:T(1024)S(1)}, f32[2048]{0:T(1024)S(1)}) all-reduce(f32[2048]{0:T(1024)S(1)} %get-tuple-element.176, f32[2048]{0:T(1024)S(1)} %get-tuple-element.177), channel_id=1, replica_groups=mesh['batch'=4,'rows'=8] {'batch'}, use_global_device_ids=true, to_apply=%region_17.18 | all-reduce | flops 4096 | bytes 32768 | tf_op jit(solution)/shard_map/psum | solution.py:63
  219.6 10.3 %fusion.6 = bf16[8,8,2048]{2,1,0:T(8,128)(2,1)} fusion(bf16[1024,2048]{1,0:T(8,128)(2,1)} %bitcast.110, f32[2048]{0:T(1024)S(1)} %copy-done.118, f32[2048]{0:T(1024)S(1)} %get-tuple-element.203, f32[1024,2048]{1,0:T(8,128)} %get-tuple-element.213, f32[2048]{0:T(1024)S(1)} %get-tuple-element.204, f32[2048]{0:T(1024)S(1)} %copy-done.20, ...), kind=kOutput, calls=%fused_computation.27 | convolution fusion | flops 297140224 | bytes 12892160 | tf_op jit(solution)/shard_map/dot_general | solution.py:167
  229.9 3.4 all-to-all-start.1
  235.3 21.5 %all-gather = bf16[8,10,512]{2,1,0:T(8,128)(2,1)S(1)} all-gather(bf16[1,10,512]{2,1,0:T(8,128)(2,1)S(1)} %fusion.14), channel_id=1, replica_groups=mesh['batch'=4,'rows'=8] {'rows'}, dimensions={0}, use_global_device_ids=true | all-gather | bytes 92160 | tf_op jit(solution)/shard_map/all_gather | solution.py:185
  258.9 14.0 %all-gather.1 = bf16[8,10,512]{2,1,0:T(8,128)(2,1)S(1)} all-gather(bf16[1,10,512]{2,1,0:T(8,128)(2,1)S(1)} %fusion.15), channel_id=1, replica_groups=mesh['batch'=4,'rows'=8] {'rows'}, dimensions={0}, use_global_device_ids=true | all-gather | bytes 92160 | tf_op jit(solution)/shard_map/all_gather | solution.py:186
  279.4 2.8 convert_reduce_fusion
  286.8 3.2 multiply_reduce_fusion.6
  293.4 4.2 fusion.20
  298.1 16.5 %all_to_all.24 = bf16[8,10,1024]{2,1,0:T(8,128)(2,1)S(1)} all-to-all(bf16[8,10,1024]{2,1,0:T(8,128)(2,1)S(1)} %reshape.231), channel_id=1, replica_groups=mesh['batch'=4,'rows'=8] {'rows'}, dimensions={0} | all-to-all | bytes 327680 | tf_op jit(solution)/shard_map/all_to_all | solution.py:32
  320.7 3.0 fusion.4
  324.5 16.6 %all_to_all.25 = bf16[8,8,2048]{2,1,0:T(8,128)(2,1)S(1)} all-to-all(bf16[8,8,2048]{2,1,0:T(8,128)(2,1)S(1)} %bitcast_select_fusion), channel_id=1, replica_groups=mesh['batch'=4,'rows'=8] {'rows'}, dimensions={0} | all-to-all | bytes 524288 | tf_op jit(solution)/shard_map/all_to_all | solution.py:244
  341.5 14.8 %fusion.44 = (f32[2048]{0:T(1024)S(1)}, f32[2048]{0:T(1024)S(1)}, f32[1024,2048]{1,0:T(8,128)}) fusion(f32[2048]{0:T(1024)S(1)} %get-tuple-element.203, f32[1024,2048]{1,0:T(8,128)} %get-tuple-element.213, f32[2048]{0:T(1024)S(1)} %get-tuple-element.204, bf16[1024,2048]{1,0:T(8,128)(2,1)} %bitcast.111, f32[2048]{0:T(1024)} %param.41, ...), kind=kOutput, calls=%fused_computation.235 | convolution fusion | flops 309587968 | bytes 21297152 | tf_op jit(solution)/shard_map/dot_general | solution.py:46
  356.3 38.3 %all-reduce.5 = (f32[2048]{0:T(1024)S(1)}, f32[2048]{0:T(1024)S(1)}) all-reduce(f32[2048]{0:T(1024)S(1)} %get-tuple-element.96, f32[2048]{0:T(1024)S(1)} %get-tuple-element.95), channel_id=1, replica_groups=mesh['batch'=4,'rows'=8] {'batch','rows'}, use_global_device_ids=true, to_apply=%region_28.29 | all-reduce | flops 4096 | bytes 32768 | tf_op jit(solution)/shard_map/psum | solution.py:247
  394.6 7.4 multiply_convert_fusion
  404.1 4.5 fusion.42
  409.1 8.1 fusion.47
  417.2 41.4 %all-reduce.4 = (f32[512]{0:T(512)S(1)}, f32[512]{0:T(512)S(1)}) all-reduce(f32[512]{0:T(512)S(1)} %get-tuple-element.102, f32[512]{0:T(512)S(1)} %get-tuple-element.101), channel_id=1, replica_groups=mesh['batch'=4,'rows'=8] {'batch','rows'}, use_global_device_ids=true, to_apply=%region_32.33 | all-reduce | flops 1024 | bytes 8192 | tf_op jit(solution)/shard_map/psum | solution.py:72
  458.6 2.8 multiply_convert_fusion.8
  465.4 6.7 copy.62
  472.1 3.6 select_maximum_fusion
  481.7 7.1 fusion.46
  488.9 52.6 %all-reduce.3 = (f32[512]{0:T(512)S(1)}, f32[512]{0:T(512)S(1)}, f32[512]{0:T(512)}, f32[512]{0:T(512)}, f32[80]{0:T(128)}) all-reduce(f32[512]{0:T(512)S(1)} %get-tuple-element.100, f32[512]{0:T(512)S(1)} %get-tuple-element.99, f32[512]{0:T(512)S(1)} %copy-done.28, ...), channel_id=1, replica_groups=mesh['batch'=4,'rows'=8] {'batch','rows'}, use_global_device_ids=true, to_apply=%region_36.37 | all-reduce | flops 2128 | bytes 17024 | tf_op jit(solution)/shard_map/psum | solution.py:72
  544.9 4.4 convolution_bitcast_fusion.2
  549.4 11.4 %fusion.57 = f32[4608,512]{1,0:T(8,128)} fusion(bf16[1024,4608]{1,0:T(8,128)(2,1)} %constant_dynamic-update-slice_fusion, bf16[1024,512]{1,0:T(8,128)(2,1)S(1)} %multiply_convert_fusion.8), kind=kOutput, calls=%fused_computation.247 | convolution fusion | flops 4831838208 | bytes 19922944 | tf_op jit(solution)/shard_map/dot_general | solution.py:46
  570.3 9.7 reduce-scatter.26.cloned.1.call-done
  581.8 49.0 %reduce-scatter.20.cloned.1.call-done = f32[256,512]{0,1:T(8,128)} async-done(((f32[2048,512]{0,1:T(8,128)}), f32[256,512]{0,1:T(8,128)}) %reduce-scatter.20.cloned.1.call-update) | async-done | bytes 524304 | tf_op jit(solution)/shard_map/reduce_scatter | solution.py:282
  632.7 98.0 %reduce-scatter.24.cloned.1.call-done = f32[576,512]{1,0:T(8,128)} async-done(((f32[4608,512]{1,0:T(8,128)}), f32[576,512]{1,0:T(8,128)}) %reduce-scatter.24.cloned.1.call-update) | async-done | bytes 1179664 | tf_op jit(solution)/shard_map/reduce_scatter | solution.py:283
  734.5 8.5 add_convert_fusion
  743.0 30.5 %all-reduce.14.cloned.1.call-done = bf16[512,80]{0,1:T(8,128)(2,1)} async-done(((bf16[512,80]{0,1:T(8,128)(2,1)}), bf16[512,80]{0,1:T(8,128)(2,1)}) %all-reduce.14.cloned.1.call-update) | async-done | bytes 81936
  774.9 26.3 %reduce-scatter.48.cloned.1.call-done = bf16[128,256]{1,0:T(8,128)(2,1)} async-done(((bf16[512,256]{1,0:T(8,128)(2,1)}), bf16[128,256]{1,0:T(8,128)(2,1)}) %reduce-scatter.48.cloned.1.call-update) | async-done | bytes 65552
  802.9 25.1 %reduce-scatter.42.cloned.1.call-done = bf16[64,512]{1,0:T(8,128)(2,1)} async-done(((bf16[64,2048]{1,0:T(8,128)(2,1)}), bf16[64,512]{1,0:T(8,128)(2,1)}) %reduce-scatter.42.cloned.1.call-update) | async-done | bytes 65552 | tf_op jit(solution)/shard_map/reduce_scatter | solution.py:310
  829.5 25.6 %reduce-scatter.34.cloned.1.call-done = bf16[256,128]{0,1:T(8,128)(2,1)} async-done(((bf16[256,512]{0,1:T(8,128)(2,1)}), bf16[256,128]{0,1:T(8,128)(2,1)}) %reduce-scatter.34.cloned.1.call-update) | async-done | bytes 65552 | tf_op jit(solution)/shard_map/reduce_scatter | solution.py:304
  856.7 25.1 %reduce-scatter.38.cloned.1.call-done = bf16[256,128]{0,1:T(8,128)(2,1)} async-done(((bf16[256,512]{0,1:T(8,128)(2,1)}), bf16[256,128]{0,1:T(8,128)(2,1)}) %reduce-scatter.38.cloned.1.call-update) | async-done | bytes 65552 | tf_op jit(solution)/shard_map/reduce_scatter | solution.py:307
  883.4 25.5 %reduce-scatter.28.cloned.1.call-done = bf16[64,512]{1,0:T(8,128)(2,1)} async-done(((bf16[64,2048]{1,0:T(8,128)(2,1)}), bf16[64,512]{1,0:T(8,128)(2,1)}) %reduce-scatter.28.cloned.1.call-update) | async-done | bytes 65552 | tf_op jit(solution)/shard_map/reduce_scatter | solution.py:298
  910.4 26.0 %reduce-scatter.22.cloned.1.call-done = bf16[256,128]{0,1:T(8,128)(2,1)} async-done(((bf16[256,512]{0,1:T(8,128)(2,1)}), bf16[256,128]{0,1:T(8,128)(2,1)}) %reduce-scatter.22.cloned.1.call-update) | async-done | bytes 65552 | tf_op jit(solution)/shard_map/reduce_scatter | solution.py:292
  938.0 27.0 %reduce-scatter.46.cloned.1.call-done = bf16[128,576]{1,0:T(8,128)(2,1)} async-done(((bf16[512,576]{1,0:T(8,128)(2,1)}), bf16[128,576]{1,0:T(8,128)(2,1)}) %reduce-scatter.46.cloned.1.call-update) | async-done | bytes 147472
  (419 shorter events, 100.3 us)
Async XLA Ops:
  7.2 226.2 %copy-start = (bf16[10,2048]{1,0:T(8,128)(2,1)S(1)}, bf16[10,2048]{1,0:T(8,128)(2,1)}, u32[]{:S(2)}) copy-start(bf16[10,2048]{1,0:T(8,128)(2,1)} %param.45) | copy-start | bytes 122884
  7.2 34.4 %all-gather.10.cloned.1.call-start = ((), (), s32[]{:S(2)}) async-start(), calls=%async_computation.19 | async-start | bytes 2359296 | tf_op jit(solution)/shard_map/all_gather | solution.py:115
  7.9 128.0 %all-gather.12.cloned.1.call-start = ((), (), s32[]{:S(2)}) async-start(), calls=%async_computation.20 | async-start | bytes 5308416 | tf_op jit(solution)/shard_map/all_gather | solution.py:116
  8.7 161.8 %all-gather.14.cloned.1.call-start = ((), (), s32[]{:S(2)}) async-start(), calls=%async_computation.21 | async-start | bytes 2359296 | tf_op jit(solution)/shard_map/all_gather | solution.py:117
  9.4 223.9 %all-gather.18.cloned.1.call-start = ((), (), s32[]{:S(2)}) async-start(), calls=%async_computation.23 | async-start | bytes 2359296 | tf_op jit(solution)/shard_map/all_gather | solution.py:119
  10.0 246.9 %all-gather.20.cloned.1.call-start = ((), (), s32[]{:S(2)}) async-start(), calls=%async_computation.24 | async-start | bytes 2359296 | tf_op jit(solution)/shard_map/all_gather | solution.py:120
  10.6 263.6 %all-gather.16.cloned.1.call-start = ((), (), s32[]{:S(2)}) async-start(), calls=%async_computation.22 | async-start | bytes 2359296 | tf_op jit(solution)/shard_map/all_gather | solution.py:118
  11.2 104.9 %all-to-all-start = ((s32[8,1,8]{2,1,0:T(1,128)}), s32[8,1,8]{2,1,0:T(1,128)S(1)}, u32[]{:S(2)}, u32[]{:S(2)}) async-start(s32[8,1,8]{2,1,0:T(1,128)} %bitcast.138), calls=%async_computation | async-start | bytes 8192 | tf_op jit(solution)/shard_map/all_to_all | solution.py:173
  17.5 259.5 %all-gather.22.cloned.1.call-start = ((), (), s32[]{:S(2)}) async-start(), calls=%async_computation.25 | async-start | bytes 2359296 | tf_op jit(solution)/shard_map/all_gather | solution.py:121
  73.2 44.1 %collective-permute-start = (bf16[64,1,16,512]{3,2,0,1:T(8,128)(2,1)S(1)}, bf16[64,1,16,512]{3,2,0,1:T(8,128)(2,1)}, u32[]{:S(2)}, u32[]{:S(2)}) collective-permute-start(bf16[64,1,16,512]{3,2,0,1:T(8,128)(2,1)S(1)} %bitcast.117), channel_id=1, source_target_pairs={{0,1},{1,2},{2,3},{3,4},{4,5},{5,6},{6,7},{8,9},{9,10},{10,11},{11... | collective-permute-start | bytes 3145736 | tf_op jit(solution)/shard_map/ppermute | solution.py:15
  75.5 41.8 %collective-permute-start.1 = (bf16[64,1,16,512]{3,2,0,1:T(8,128)(2,1)S(1)}, bf16[64,1,16,512]{3,2,0,1:T(8,128)(2,1)}, u32[]{:S(2)}, u32[]{:S(2)}) collective-permute-start(bf16[64,1,16,512]{3,2,0,1:T(8,128)(2,1)S(1)} %bitcast.118), channel_id=1, source_target_pairs={{1,0},{2,1},{3,2},{4,3},{5,4},{6,5},{7,6},{9,8},{10,9},{11,10},{12... | collective-permute-start | bytes 3145736 | tf_op jit(solution)/shard_map/ppermute | solution.py:17
  77.4 141.7 %copy-start.35 = (s32[64]{0:T(128)}, s32[64]{0:T(128)S(1)}, u32[]{:S(2)}) copy-start(s32[64]{0:T(128)S(1)} %get-tuple-element.149) | copy-start | bytes 772
  77.4 141.7 %copy-start.37 = (s32[64]{0:T(128)}, s32[64]{0:T(128)S(1)}, u32[]{:S(2)}) copy-start(s32[64]{0:T(128)S(1)} %get-tuple-element.150) | copy-start | bytes 772
  77.4 141.7 %copy-start.39 = (s32[64]{0:T(128)}, s32[64]{0:T(128)S(1)}, u32[]{:S(2)}) copy-start(s32[64]{0:T(128)S(1)} %get-tuple-element.151) | copy-start | bytes 772
  77.5 141.7 %copy-start.41 = (s32[64]{0:T(128)}, s32[64]{0:T(128)S(1)}, u32[]{:S(2)}) copy-start(s32[64]{0:T(128)S(1)} %get-tuple-element.152) | copy-start | bytes 772
  77.5 141.7 %copy-start.43 = (s32[64]{0:T(128)}, s32[64]{0:T(128)S(1)}, u32[]{:S(2)}) copy-start(s32[64]{0:T(128)S(1)} %get-tuple-element.153) | copy-start | bytes 772
  77.5 141.7 %copy-start.45 = (s32[64]{0:T(128)}, s32[64]{0:T(128)S(1)}, u32[]{:S(2)}) copy-start(s32[64]{0:T(128)S(1)} %get-tuple-element.154) | copy-start | bytes 772
  77.5 141.7 %copy-start.47 = (s32[64]{0:T(128)}, s32[64]{0:T(128)S(1)}, u32[]{:S(2)}) copy-start(s32[64]{0:T(128)S(1)} %get-tuple-element.155) | copy-start | bytes 772
  77.5 141.7 %copy-start.49 = (s32[64]{0:T(128)}, s32[64]{0:T(128)S(1)}, u32[]{:S(2)}) copy-start(s32[64]{0:T(128)S(1)} %get-tuple-element.156) | copy-start | bytes 772
  77.5 141.7 %copy-start.51 = (s32[64]{0:T(128)}, s32[64]{0:T(128)S(1)}, u32[]{:S(2)}) copy-start(s32[64]{0:T(128)S(1)} %get-tuple-element.157) | copy-start | bytes 772
  78.7 140.5 %copy-start.83 = (s32[64]{0:T(128)}, s32[64]{0:T(128)S(1)}, u32[]{:S(2)}) copy-start(s32[64]{0:T(128)S(1)} %get-tuple-element.116) | copy-start | bytes 772
  78.7 140.5 %copy-start.85 = (s32[64]{0:T(128)}, s32[64]{0:T(128)S(1)}, u32[]{:S(2)}) copy-start(s32[64]{0:T(128)S(1)} %get-tuple-element.117) | copy-start | bytes 772
  78.7 140.5 %copy-start.87 = (s32[64]{0:T(128)}, s32[64]{0:T(128)S(1)}, u32[]{:S(2)}) copy-start(s32[64]{0:T(128)S(1)} %get-tuple-element.118) | copy-start | bytes 772
  78.8 140.5 %copy-start.89 = (s32[64]{0:T(128)}, s32[64]{0:T(128)S(1)}, u32[]{:S(2)}) copy-start(s32[64]{0:T(128)S(1)} %get-tuple-element.119) | copy-start | bytes 772
  78.8 140.5 %copy-start.91 = (s32[64]{0:T(128)}, s32[64]{0:T(128)S(1)}, u32[]{:S(2)}) copy-start(s32[64]{0:T(128)S(1)} %get-tuple-element.120) | copy-start | bytes 772
  78.8 140.5 %copy-start.93 = (s32[64]{0:T(128)}, s32[64]{0:T(128)S(1)}, u32[]{:S(2)}) copy-start(s32[64]{0:T(128)S(1)} %get-tuple-element.121) | copy-start | bytes 772
  229.9 43.0 %all-to-all-start.1 = ((bf16[8,8,2048]{2,1,0:T(8,128)(2,1)}), bf16[8,8,2048]{2,1,0:T(8,128)(2,1)S(1)}, u32[]{:S(2)}, u32[]{:S(2)}) async-start(bf16[8,8,2048]{2,1,0:T(8,128)(2,1)} %fusion.6), calls=%async_computation.1 | async-start | bytes 524288 | tf_op jit(solution)/shard_map/all_to_all | solution.py:172
  233.3 327.6 %reduce-scatter.44.cloned.1.call-start = ((), (), s32[]{:S(2)}) async-start(), calls=%async_computation.38 | async-start | bytes 1474560 | tf_op jit(solution)/shard_map/reduce_scatter | solution.py:289
  283.7 278.9 %reduce-scatter.30.cloned.1.call-start = ((), (), s32[]{:S(2)}) async-start(), calls=%async_computation.31 | async-start | bytes 4718592 | tf_op jit(solution)/shard_map/reduce_scatter | solution.py:285
  293.4 271.2 %reduce-scatter.40.cloned.1.call-start = ((), (), s32[]{:S(2)}) async-start(), calls=%async_computation.36 | async-start | bytes 4718592 | tf_op jit(solution)/shard_map/reduce_scatter | solution.py:288
  297.6 268.8 %reduce-scatter.32.cloned.1.call-start = ((), (), s32[]{:S(2)}) async-start(), calls=%async_computation.32 | async-start | bytes 4718592 | tf_op jit(solution)/shard_map/reduce_scatter | solution.py:286
  317.4 251.1 %reduce-scatter.36.cloned.1.call-start = ((), (), s32[]{:S(2)}) async-start(), calls=%async_computation.34 | async-start | bytes 4718592 | tf_op jit(solution)/shard_map/reduce_scatter | solution.py:287
  320.5 259.5 %reduce-scatter.26.cloned.1.call-start = ((), (), s32[]{:S(2)}) async-start(), calls=%async_computation.29 | async-start | bytes 4718592 | tf_op jit(solution)/shard_map/reduce_scatter | solution.py:284
  408.6 222.2 %reduce-scatter.20.cloned.1.call-start = ((), (), s32[]{:S(2)}) async-start(), calls=%async_computation.26 | async-start | bytes 4718592 | tf_op jit(solution)/shard_map/reduce_scatter | solution.py:282
  461.4 10.7 %collective-permute-start.2 = (bf16[64,1,16,512]{3,2,0,1:T(8,128)(2,1)S(1)}, bf16[64,1,16,512]{3,2,0,1:T(8,128)(2,1)}, u32[]{:S(2)}, u32[]{:S(2)}) collective-permute-start(bf16[64,1,16,512]{3,2,0,1:T(8,128)(2,1)S(1)} %bitcast.106), channel_id=1, source_target_pairs={{0,1},{1,2},{2,3},{3,4},{4,5},{5,6},{6,7},{8,9},{9,10},{10,11},{11... | collective-permute-start | bytes 3145736 | tf_op jit(solution)/shard_map/ppermute | solution.py:15
  464.1 8.0 collective-permute-start.3
  549.3 181.4 %reduce-scatter.24.cloned.1.call-start = ((), (), s32[]{:S(2)}) async-start(), calls=%async_computation.28 | async-start | bytes 10616832 | tf_op jit(solution)/shard_map/reduce_scatter | solution.py:283
  560.8 212.7 %all-reduce.14.cloned.1.call-start = ((), (), s32[]{:S(2)}) async-start(), calls=%async_computation.41 | async-start | bytes 163840
  562.5 238.7 %reduce-scatter.48.cloned.1.call-start = ((), (), s32[]{:S(2)}) async-start(), calls=%async_computation.40 | async-start | bytes 327680
  564.5 263.5 %reduce-scatter.42.cloned.1.call-start = ((), (), s32[]{:S(2)}) async-start(), calls=%async_computation.37 | async-start | bytes 327680 | tf_op jit(solution)/shard_map/reduce_scatter | solution.py:310
  566.4 166.8 %copy-start.123 = (u32[32]{0:T(128)S(1)}, u32[32]{0:T(128)}, u32[]{:S(2)}) copy-start(u32[32]{0:T(128)} %constant.85) | copy-start | bytes 388
  566.4 168.1 %copy-start.5 = (bf16[1024,512]{1,0:T(8,128)(2,1)S(1)}, bf16[1024,512]{1,0:T(8,128)(2,1)}, u32[]{:S(2)}) copy-start(bf16[1024,512]{1,0:T(8,128)(2,1)} %copy-done.4) | copy-start | bytes 3145732
  566.4 288.7 %reduce-scatter.34.cloned.1.call-start = ((), (), s32[]{:S(2)}) async-start(), calls=%async_computation.33 | async-start | bytes 327680 | tf_op jit(solution)/shard_map/reduce_scatter | solution.py:304
  568.4 313.4 %reduce-scatter.38.cloned.1.call-start = ((), (), s32[]{:S(2)}) async-start(), calls=%async_computation.35 | async-start | bytes 327680 | tf_op jit(solution)/shard_map/reduce_scatter | solution.py:307
  570.3 338.6 %reduce-scatter.28.cloned.1.call-start = ((), (), s32[]{:S(2)}) async-start(), calls=%async_computation.30 | async-start | bytes 327680 | tf_op jit(solution)/shard_map/reduce_scatter | solution.py:298
  581.8 354.6 %reduce-scatter.22.cloned.1.call-start = ((), (), s32[]{:S(2)}) async-start(), calls=%async_computation.27 | async-start | bytes 327680 | tf_op jit(solution)/shard_map/reduce_scatter | solution.py:292
  632.7 332.3 %reduce-scatter.46.cloned.1.call-start = ((), (), s32[]{:S(2)}) async-start(), calls=%async_computation.39 | async-start | bytes 819200
  734.5 232.3 %copy-start.1 = (bf16[10,2048]{1,0:T(8,128)(2,1)S(1)}, bf16[10,2048]{1,0:T(8,128)(2,1)}, u32[]{:S(2)}) copy-start(bf16[10,2048]{1,0:T(8,128)(2,1)} %param.45) | copy-start | bytes 122884
  (107 other events, 4540.1 us)
Sparse Core Ops, SparseCore 0:
  9.6 31.8 all-gather.9
  43.2 55.0 all-gather.11
  99.9 33.1 all-gather.13
  134.6 28.8 all-gather.17
  165.0 28.9 all-gather.19
  195.4 28.6 all-gather.15
  225.7 35.8 all-gather.21
  283.8 32.4 reduce-scatter.43
  318.6 54.1 reduce-scatter.29
  375.0 49.0 reduce-scatter.39
  426.4 51.2 reduce-scatter.31
  479.9 49.4 reduce-scatter.35
  531.7 48.2 reduce-scatter.25
  582.7 48.1 reduce-scatter.19
  633.0 97.6 reduce-scatter.23
  734.1 39.4 all-reduce.13
  776.4 24.8 reduce-scatter.47
  803.8 24.0 reduce-scatter.41
  831.0 24.0 reduce-scatter.33
  857.7 24.0 reduce-scatter.37
  884.8 24.0 reduce-scatter.27
  912.2 24.0 reduce-scatter.21
  939.5 25.3 reduce-scatter.45
